TPU v7x, 32 devices: a whole 2x2x4 slice. The times are simulated.
32 devices in a mesh: rows: 8 (over y, x, core), sub: 4 (over z).
Axes of the slice: x: 2, y: 2, z: 4, core: 2. Of those that a mesh axis runs over, the one named last changes fastest.
Arguments:
- old_basis: bfloat16 [32, 524288], P(None, ('rows', 'sub')), may hold values from -1 to 1
- snapshots: bfloat16 [512, 524288], P(None, ('rows', 'sub')), may hold values from -16 to 16
- gap_flags: int32 [512, 4096], P(None, ('rows', 'sub')), may hold values from 0 to 1, as said below
- sketch_seed: int32 [512, 64], replicated, may hold values from -1 to 1
Outputs:
- new_basis: float32 [32, 524288], P(None, ('rows', 'sub'))
- coefficients: float32 [32, 512], replicated
Inputs may be any that keep to these rules, and one draw needn't show every extreme that they name: `gap_flags`: 1 marks a block of 128 velocity rows measured in that snapshot, 0 a gap; every snapshot has measured blocks and gaps.
All inputs are finite; a program needn't handle non-finite values.
Results may differ from a plain program's by a relative error of at most 0.00135.
The roundings to bfloat16 on the way count: a program that leaves them out, or rounds other values in their place, can miss the bound.
Values may be sent and summed in bfloat16 or wider, within the bound.
No kernel may reach another device: no remote copies, remote signals or barrier semaphores. Data moves between devices by JAX's collectives and lax.ppermute only.
A program may use at most 192 MiB of HBM per device.

v0:
```python
import math
import jax
import jax.numpy as jnp
from jax import lax
from jax.sharding import PartitionSpec as P

POWER = 2
damping = 0.005
highest = lax.Precision.HIGHEST


def cholesky_last(system):
    extent = system.shape[0]
    factor = jnp.zeros_like(system)
    for column in range(extent):
        partial_sum = jnp.sum(factor * factor[column : column + 1], axis=1)
        remain = system[:, column] - partial_sum
        diagonal_root = jnp.sqrt(remain[column])
        lower_part = (jnp.arange(extent) >= column).reshape((extent,) + (1,) * (system.ndim - 2))
        factor = factor.at[:, column].set(jnp.where(lower_part, remain / diagonal_root, 0.0))
    return factor


def lower_solve(factor, target):
    extent = factor.shape[0]
    result = jnp.zeros_like(target)
    for column in range(extent):
        current = (target[column] - jnp.sum(factor[column] * result, axis=0)) / factor[
            column, column
        ]
        result = result.at[column].set(current)
    return result


def upper_solve(factor, target):
    extent = factor.shape[0]
    result = jnp.zeros_like(target)
    for column in reversed(range(extent)):
        current = (target[column] - jnp.sum(factor[:, column] * result, axis=0)) / factor[
            column, column
        ]
        result = result.at[column].set(current)
    return result


def solve_normal(grams, right, modes, rows_all):
    snapshot_count = grams.shape[0]
    identity = jnp.eye(modes, dtype=jnp.float32)[:, :, None]
    system = grams.T.reshape(modes, modes, snapshot_count) + damping * rows_all * identity
    factor = cholesky_last(system)
    return upper_solve(factor, lower_solve(factor, right.T))


def inverse_factor(products):
    extent = products.shape[0]
    factor = cholesky_last(products[:, :, None])
    return lower_solve(factor, jnp.eye(extent, dtype=jnp.float32))


def mask_blocks(samples, flag_blocks):
    snapshot_count, blocks_dev = flag_blocks.shape
    weights = flag_blocks.astype(samples.dtype)[:, :, None]
    return (samples.reshape(snapshot_count, blocks_dev, -1) * weights).reshape(snapshot_count, -1)


def refill(samples, flag_blocks, recon_low):
    snapshot_count, blocks_dev = flag_blocks.shape
    observed = (flag_blocks > 0)[:, :, None]
    combined = jnp.where(
        observed,
        samples.reshape(snapshot_count, blocks_dev, -1),
        recon_low.reshape(snapshot_count, blocks_dev, -1),
    )
    return combined.reshape(snapshot_count, -1)


def contract_rows(former, latter):
    return lax.dot_general(
        former, latter, (((1,), (1,)), ((), ())), preferred_element_type=jnp.float32
    )


def contract_first(former, latter):
    return lax.dot_general(
        former, latter, (((0,), (0,)), ((), ())), preferred_element_type=jnp.float32
    )


def per_device(old_basis, snapshots, gap_flags, sketch_seed):
    modes = old_basis.shape[0]
    rows_all = old_basis.shape[1] * lax.axis_size(("rows", "sub"))
    blocks_dev = gap_flags.shape[1]
    masked = mask_blocks(snapshots, gap_flags)
    right = contract_rows(masked, old_basis)
    pieces = old_basis.reshape(modes, blocks_dev, -1)
    block_grams = jnp.einsum("kbi,lbi->bkl", pieces, pieces, preferred_element_type=jnp.float32)
    block_rows = block_grams.reshape(blocks_dev, modes * modes)
    grams = jnp.dot(gap_flags.astype(jnp.float32), block_rows, precision=highest)
    mixer = sketch_seed.astype(jnp.bfloat16)
    gram_total, right_total = lax.psum((grams, right), ("rows", "sub"))
    coefficients = solve_normal(gram_total, right_total, modes, rows_all)
    recon_low = contract_first(coefficients.astype(jnp.bfloat16), old_basis).astype(jnp.bfloat16)
    filled = refill(snapshots, gap_flags, recon_low)
    sketch = contract_first(mixer, filled)
    inverse = None
    for sweep_index in range(POWER + 1):
        if sweep_index > 0:
            sketch = contract_first(mixer, filled)
        local_gram = lax.dot_general(
            sketch,
            sketch,
            (((1,), (1,)), ((), ())),
            precision=highest,
            preferred_element_type=jnp.float32,
        )
        products = lax.psum(local_gram, ("rows", "sub"))
        inverse = inverse_factor(products)
        if sweep_index < POWER:
            ortho_rows = jnp.dot(inverse, sketch, precision=highest).astype(jnp.bfloat16)
            mixer_share = lax.psum_scatter(
                contract_rows(filled, ortho_rows), ("rows", "sub"), scatter_dimension=0, tiled=True
            ).astype(jnp.bfloat16)
            mixer = lax.all_gather(mixer_share, ("rows", "sub"), axis=0, tiled=True)
    root_rows = math.sqrt(rows_all)
    new_basis = jnp.dot(inverse[:modes], sketch, precision=highest) * root_rows
    return (new_basis, coefficients)


def solution(mesh):
    in_specs = (P(None, ("rows", "sub")), P(None, ("rows", "sub")), P(None, ("rows", "sub")), P())
    out_specs = (P(None, ("rows", "sub")), P())
    return jax.shard_map(
        per_device, mesh=mesh, in_specs=in_specs, out_specs=out_specs, check_vma=False
    )
```

profile of v0, /device:TPU:0, one launch (start us, length us, event | category | flops | bytes accessed | tf_op | source)
XLA Modules:
  0.0 1549.7 jit_solution(17264317991794373059)
XLA Ops:
  9.1 2.1 copy.518
  11.2 2.8 fusion.6
  14.1 2.5 copy.519
  16.6 13.0 mul.4308
  29.6 24.4 %fusion.2 = f32[32,512]{1,0:T(8,128)} fusion(bf16[32,16384]{1,0:T(8,128)(2,1)S(1)} %copy-done, bf16[512,16384]{1,0:T(8,128)(2,1)} %param.965, bf16[64,8,128,128]{3,2,1,0:T(8,128)(2,1)} %bitcast.3922), kind=kOutput, calls=%fused_computation.40 | convolution fusion | flops 545259520 | bytes 34668544 | tf_op jit(solution)/shard_map/dot_general | solution.py:78
  54.7 137.0 %all-reduce.12.cloned.1.call-done = (f32[32,32,512]{2,0,1:T(8,128)}, f32[32,512]{1,0:T(8,128)}) async-done(((f32[32,32,512]{2,0,1:T(8,128)}, f32[32,512]{1,0:T(8,128)}), (f32[32,32,512]{2,0,1:T(8,128)}, f32[32,512]{1,0:T(8,128)})) %all-reduce.12.cloned.1.call-update) | async-done | bytes 2162704 | tf_op jit(solution)/shard_map/psum | solution.py:100
  191.7 1.8 broadcast_add_fusion
  291.6 12.0 broadcast_in_dim.635
  303.5 15.2 bitcast_select_fusion
  318.8 8.8 fusion.224
  327.6 1.9 copy-done.5
  329.5 3.4 convolution_bitcast_fusion.2
  332.9 39.6 %psum.37 = f32[64,64,1]{1,0,2:T(8,128)S(1)} all-reduce(f32[64,64,1]{1,0,2:T(8,128)S(1)} %convolution_bitcast_fusion.2), channel_id=1, replica_groups=mesh['rows'=8,'sub'=4] {'rows','sub'}, use_global_device_ids=true, to_apply=%region_97.98 | all-reduce | flops 4096 | bytes 32768 | tf_op jit(solution)/shard_map/psum | solution.py:116
  498.8 1.4 fusion.505
  500.2 1.4 fusion.504
  510.2 1.4 fusion.497
  511.7 1.4 fusion.496
  516.1 1.4 fusion.493
  530.4 1.4 fusion.483
  537.6 1.4 fusion.478
  566.0 1.4 fusion.458
  578.8 1.4 fusion.449
  581.6 6.0 convolution_convert_fusion.2
  587.6 8.8 fusion.526
  596.5 133.4 %reduce-scatter.3.cloned.1.call-done = f32[16,64]{1,0:T(8,128)} async-done(((f32[512,64]{1,0:T(8,128)}), f32[16,64]{1,0:T(8,128)}) %reduce-scatter.3.cloned.1.call-update) | async-done | bytes 4112 | tf_op jit(solution)/shard_map/reduce_scatter | solution.py:120
  730.6 64.8 %all_gather.6 = bf16[512,64]{1,0:T(8,128)(2,1)S(1)} all-gather(bf16[16,64]{1,0:T(8,128)(2,1)S(1)} %convert_element_type.415), channel_id=1, replica_groups=mesh['rows'=8,'sub'=4] {'rows','sub'}, dimensions={0}, use_global_device_ids=true | all-gather | bytes 67584 | tf_op jit(solution)/shard_map/all_gather | solution.py:123
  795.3 8.9 fusion.527
  804.2 1.9 copy-done.4
  806.2 3.4 convolution_bitcast_fusion.1
  809.6 39.9 %psum.38 = f32[64,64,1]{1,0,2:T(8,128)S(1)} all-reduce(f32[64,64,1]{1,0,2:T(8,128)S(1)} %convolution_bitcast_fusion.1), channel_id=1, replica_groups=mesh['rows'=8,'sub'=4] {'rows','sub'}, use_global_device_ids=true, to_apply=%region_226.227 | all-reduce | flops 4096 | bytes 32768 | tf_op jit(solution)/shard_map/psum | solution.py:116
  970.7 1.9 subtract_divide_fusion.3
  972.7 1.4 fusion.447
  974.2 1.4 fusion.446
  979.9 1.4 fusion.442
  981.4 1.4 fusion.441
  991.3 1.4 fusion.434
  997.2 1.4 fusion.430
  1011.5 1.4 fusion.420
  1018.7 1.4 fusion.415
  1047.1 1.4 fusion.395
  1059.9 1.4 fusion.386
  1062.7 6.0 convolution_convert_fusion.1
  1068.7 8.8 fusion.528
  1077.5 133.0 %reduce-scatter.5.cloned.1.call-done = f32[16,64]{1,0:T(8,128)} async-done(((f32[512,64]{1,0:T(8,128)}), f32[16,64]{1,0:T(8,128)}) %reduce-scatter.5.cloned.1.call-update) | async-done | bytes 4112 | tf_op jit(solution)/shard_map/reduce_scatter | solution.py:120
  1211.2 64.8 %all_gather.7 = bf16[512,64]{1,0:T(8,128)(2,1)S(1)} all-gather(bf16[16,64]{1,0:T(8,128)(2,1)S(1)} %convert_element_type.417), channel_id=1, replica_groups=mesh['rows'=8,'sub'=4] {'rows','sub'}, dimensions={0}, use_global_device_ids=true | all-gather | bytes 67584 | tf_op jit(solution)/shard_map/all_gather | solution.py:123
  1276.0 8.9 fusion.529
  1284.9 1.9 copy-done.3
  1286.8 3.4 convolution_bitcast_fusion
  1290.2 39.9 %psum.39 = f32[64,64,1]{1,0,2:T(8,128)S(1)} all-reduce(f32[64,64,1]{1,0,2:T(8,128)S(1)} %convolution_bitcast_fusion), channel_id=1, replica_groups=mesh['rows'=8,'sub'=4] {'rows','sub'}, use_global_device_ids=true, to_apply=%region_355.356 | all-reduce | flops 4096 | bytes 32768 | tf_op jit(solution)/shard_map/psum | solution.py:116
  1450.6 1.9 subtract_divide_fusion.2
  1452.6 1.4 fusion.384
  1455.5 1.4 fusion.382
  1462.7 1.4 fusion.377
  1467.0 1.4 fusion.374
  1468.5 1.4 fusion.373
  1471.4 1.4 fusion.371
  1482.8 1.4 fusion.363
  1484.2 1.4 fusion.362
  1498.5 1.4 fusion.352
  1508.6 1.4 fusion.345
  1520.1 1.4 fusion.337
  1530.0 1.4 fusion.330
  1532.9 1.4 fusion.328
  1537.1 5.7 convolution_multiply_fusion
  (2302 shorter events, 543.1 us)
Async XLA Ops:
  7.2 1.3 copy-start
  7.2 184.5 %all-reduce.12.cloned.1.call-start = ((), (), s32[]{:S(2)}) async-start(), calls=%async_computation.4 | async-start | bytes 4325376 | tf_op jit(solution)/shard_map/psum | solution.py:100
  9.1 2.1 copy-start.8
  54.0 675.8 %reduce-scatter.3.cloned.1.call-start = ((), (), s32[]{:S(2)}) async-start(), calls=%async_computation.2 | async-start | bytes 270336 | tf_op jit(solution)/shard_map/reduce_scatter | solution.py:120
  54.7 443.3 %copy-start.9 = (f32[64,64]{1,0:T(8,128)}, f32[64,64]{1,0:T(8,128)S(1)}, u32[]{:S(2)}) copy-start(f32[64,64]{1,0:T(8,128)S(1)} %fusion.228) | copy-start | bytes 49156
  210.1 2.8 copy-start.2
  238.2 3.3 copy-start.6
  291.5 12.0 copy-start.7
  303.5 15.2 copy-start.10
  327.5 1.9 copy-start.5
  596.4 614.1 %reduce-scatter.5.cloned.1.call-start = ((), (), s32[]{:S(2)}) async-start(), calls=%async_computation.3 | async-start | bytes 270336 | tf_op jit(solution)/shard_map/reduce_scatter | solution.py:120
  804.2 1.9 copy-start.4
  1284.9 1.9 copy-start.3
  1537.0 5.7 copy-start.1
Sparse Core Ops, SparseCore 0:
  54.2 137.4 all-reduce.11
  596.5 133.2 reduce-scatter.2
  1077.6 132.8 reduce-scatter.4
where the time goes:
time: 1580 us; the launch traced here: 1550 us
  waiting for transfers between devices  403 us (26%)
  other arithmetic  392 us (25%)
  blocking collectives  249 us (16%)
  local copies, waits for them, and re-layouts  234 us (15%)
  between operations  155 us (10%)
  matrix products  115 us (7%)
    div x219, other arithmetic, lower_solve(): (target[column] - jnp.sum(factor[column] * result, axis=0)) / factor[colu...  267 us
    reduce_scatter x2, waiting for transfers between devices, per_device(): lax.psum_scatter(contract_rows(filled, ortho_rows), ('rows', 'sub'), scat...  266 us
    psum x1, waiting for transfers between devices, per_device(): gram_total, right_total = lax.psum((grams, right), ('rows', 'sub'))  137 us
    all_gather x2, blocking collectives, per_device(): mixer = lax.all_gather(mixer_share, ('rows', 'sub'), axis=0, tiled=True)  130 us
    psum x3, blocking collectives, per_device(): products = lax.psum(local_gram, ('rows', 'sub'))  119 us
    slice x192, local copies, waits for them, and re-layouts, cholesky_last(): diagonal_root = jnp.sqrt(remain[column])  113 us
    dot_general x3, matrix products, contract_rows(): lax.dot_general(former, latter, (((1,), (1,)), ((), ())), preferred_eleme...  42 us
    dot_general x4, matrix products, contract_first(): lax.dot_general(former, latter, (((0,), (0,)), ((), ())), preferred_eleme...  41.8 us
  transfers between devices with their start and end apart: 3, of which 3 were waited for; matrix products, arithmetic and copies ran while one was open for 0% of the time, Pallas kernels for 0%

commit v1 on v0

--- a/solution.py
+++ b/solution.py
@@ -113,7 +113,7 @@
             precision=highest,
             preferred_element_type=jnp.float32,
         )
-        products = lax.psum(local_gram, ("rows", "sub"))
+        products = jnp.sum(lax.all_gather(local_gram, ("rows", "sub")), axis=0)
         inverse = inverse_factor(products)
         if sweep_index < POWER:
             ortho_rows = jnp.dot(inverse, sketch, precision=highest).astype(jnp.bfloat16)

time: 1580 us -> 1670 us (1.057)
  blocking collectives: 249 us -> 353 us
    all_gather x0 -> x3, blocking collectives: none -> 224 us  [per_device(): products = jnp.sum(lax.all_gather(local_gram, ('rows', 'sub')), axis=0)]
    psum x3 -> x0, blocking collectives: 119 us -> none  [per_device(): products = lax.psum(local_gram, ('rows', 'sub'))]
where the time goes in v1:
time: 1670 us; the launch traced here: 1640 us
  waiting for transfers between devices  399 us (24%)
  other arithmetic  393 us (24%)
  blocking collectives  353 us (21%)
  local copies, waits for them, and re-layouts  229 us (14%)
  between operations  155 us (9%)
  matrix products  115 us (7%)
    div x219, other arithmetic, lower_solve(): (target[column] - jnp.sum(factor[column] * result, axis=0)) / factor[colu...  267 us
    reduce_scatter x2, waiting for transfers between devices, per_device(): lax.psum_scatter(contract_rows(filled, ortho_rows), ('rows', 'sub'), scat...  262 us
    all_gather x3, blocking collectives, per_device(): products = jnp.sum(lax.all_gather(local_gram, ('rows', 'sub')), axis=0)  224 us
    psum x1, waiting for transfers between devices, per_device(): gram_total, right_total = lax.psum((grams, right), ('rows', 'sub'))  137 us
    all_gather x2, blocking collectives, per_device(): mixer = lax.all_gather(mixer_share, ('rows', 'sub'), axis=0, tiled=True)  130 us
    slice x192, local copies, waits for them, and re-layouts, cholesky_last(): diagonal_root = jnp.sqrt(remain[column])  113 us
    dot_general x3, matrix products, contract_rows(): lax.dot_general(former, latter, (((1,), (1,)), ((), ())), preferred_eleme...  42 us
    dot_general x4, matrix products, contract_first(): lax.dot_general(former, latter, (((0,), (0,)), ((), ())), preferred_eleme...  41.8 us
  transfers between devices with their start and end apart: 3, of which 3 were waited for; matrix products, arithmetic and copies ran while one was open for 0% of the time, Pallas kernels for 0%

profile of v1, /device:TPU:0, one launch (start us, length us, event | category | flops | bytes accessed | tf_op | source)
XLA Modules:
  0.0 1644.3 jit_solution(8783778420193226714)
XLA Ops:
  9.1 2.1 copy.652
  11.2 2.8 fusion.6
  14.1 2.5 copy.653
  16.6 13.0 mul.4308
  29.6 24.4 %fusion.2 = f32[32,512]{1,0:T(8,128)} fusion(bf16[32,16384]{1,0:T(8,128)(2,1)S(1)} %copy-done, bf16[512,16384]{1,0:T(8,128)(2,1)} %param.965, bf16[64,8,128,128]{3,2,1,0:T(8,128)(2,1)} %bitcast.4126), kind=kOutput, calls=%fused_computation.40 | convolution fusion | flops 545259520 | bytes 34668544 | tf_op jit(solution)/shard_map/dot_general | solution.py:78
  54.7 137.0 %all-reduce.12.cloned.1.call-done = (f32[32,32,512]{2,0,1:T(8,128)}, f32[32,512]{1,0:T(8,128)}) async-done(((f32[32,32,512]{2,0,1:T(8,128)}, f32[32,512]{1,0:T(8,128)}), (f32[32,32,512]{2,0,1:T(8,128)}, f32[32,512]{1,0:T(8,128)})) %all-reduce.12.cloned.1.call-update) | async-done | bytes 2162704 | tf_op jit(solution)/shard_map/psum | solution.py:100
  191.7 1.8 broadcast_add_fusion
  291.5 12.0 broadcast_in_dim.635
  303.5 15.2 bitcast_select_fusion
  318.6 8.8 fusion.224
  327.4 3.4 fusion.526
  330.8 75.7 %all-gather = f32[2048,64]{1,0:T(8,128)S(1)} all-gather(f32[64,64]{1,0:T(8,128)S(1)} %fusion.526), channel_id=2, replica_groups=mesh['rows'=8,'sub'=4] {'rows','sub'}, dimensions={0}, use_global_device_ids=true | all-gather | bytes 540672 | tf_op jit(solution)/shard_map/all_gather | solution.py:116
  532.9 1.4 fusion.505
  534.4 1.4 fusion.504
  544.4 1.4 fusion.497
  545.9 1.4 fusion.496
  550.2 1.4 fusion.493
  564.6 1.4 fusion.483
  571.8 1.4 fusion.478
  600.2 1.4 fusion.458
  613.0 1.4 fusion.449
  615.8 6.0 convolution_convert_fusion.2
  621.8 8.8 fusion.527
  630.7 131.0 %reduce-scatter.3.cloned.1.call-done = f32[16,64]{1,0:T(8,128)} async-done(((f32[512,64]{1,0:T(8,128)}), f32[16,64]{1,0:T(8,128)}) %reduce-scatter.3.cloned.1.call-update) | async-done | bytes 4112 | tf_op jit(solution)/shard_map/reduce_scatter | solution.py:120
  762.4 64.8 %all_gather.26 = bf16[512,64]{1,0:T(8,128)(2,1)S(1)} all-gather(bf16[16,64]{1,0:T(8,128)(2,1)S(1)} %convert_element_type.415), channel_id=1, replica_groups=mesh['rows'=8,'sub'=4] {'rows','sub'}, dimensions={0}, use_global_device_ids=true | all-gather | bytes 67584 | tf_op jit(solution)/shard_map/all_gather | solution.py:123
  827.2 8.9 fusion.528
  836.1 3.4 fusion.529
  839.5 74.1 %all-gather.1 = f32[2048,64]{1,0:T(8,128)S(1)} all-gather(f32[64,64]{1,0:T(8,128)S(1)} %fusion.529), channel_id=3, replica_groups=mesh['rows'=8,'sub'=4] {'rows','sub'}, dimensions={0}, use_global_device_ids=true | all-gather | bytes 540672 | tf_op jit(solution)/shard_map/all_gather | solution.py:116
  1034.9 1.9 subtract_divide_fusion.3
  1036.9 1.4 fusion.447
  1038.4 1.4 fusion.446
  1044.1 1.4 fusion.442
  1045.6 1.4 fusion.441
  1055.6 1.4 fusion.434
  1057.1 1.4 fusion.433
  1061.4 1.4 fusion.430
  1075.7 1.4 fusion.420
  1082.9 1.4 fusion.415
  1111.4 1.4 fusion.395
  1124.1 1.4 fusion.386
  1126.9 6.0 convolution_convert_fusion.1
  1132.9 8.8 fusion.530
  1141.7 131.0 %reduce-scatter.5.cloned.1.call-done = f32[16,64]{1,0:T(8,128)} async-done(((f32[512,64]{1,0:T(8,128)}), f32[16,64]{1,0:T(8,128)}) %reduce-scatter.5.cloned.1.call-update) | async-done | bytes 4112 | tf_op jit(solution)/shard_map/reduce_scatter | solution.py:120
  1273.4 64.7 %all_gather.29 = bf16[512,64]{1,0:T(8,128)(2,1)S(1)} all-gather(bf16[16,64]{1,0:T(8,128)(2,1)S(1)} %convert_element_type.417), channel_id=1, replica_groups=mesh['rows'=8,'sub'=4] {'rows','sub'}, dimensions={0}, use_global_device_ids=true | all-gather | bytes 67584 | tf_op jit(solution)/shard_map/all_gather | solution.py:123
  1338.1 8.9 fusion.531
  1347.1 3.4 fusion.532
  1350.5 74.1 %all-gather.2 = f32[2048,64]{1,0:T(8,128)S(1)} all-gather(f32[64,64]{1,0:T(8,128)S(1)} %fusion.532), channel_id=4, replica_groups=mesh['rows'=8,'sub'=4] {'rows','sub'}, dimensions={0}, use_global_device_ids=true | all-gather | bytes 540672 | tf_op jit(solution)/shard_map/all_gather | solution.py:116
  1545.1 1.9 subtract_divide_fusion.2
  1547.1 1.4 fusion.384
  1550.1 1.4 fusion.382
  1557.3 1.4 fusion.377
  1561.6 1.4 fusion.374
  1563.1 1.4 fusion.373
  1565.9 1.4 fusion.371
  1574.5 1.4 fusion.365
  1577.3 1.4 fusion.363
  1578.8 1.4 fusion.362
  1593.1 1.4 fusion.352
  1600.3 1.4 fusion.347
  1603.2 1.4 fusion.345
  1614.6 1.4 fusion.337
  1624.6 1.4 fusion.330
  1627.5 1.4 fusion.328
  1631.6 5.7 convolution_multiply_fusion
  (2305 shorter events, 539.3 us)
Async XLA Ops:
  7.2 1.3 copy-start
  7.2 184.5 %all-reduce.12.cloned.1.call-start = ((), (), s32[]{:S(2)}) async-start(), calls=%async_computation.4 | async-start | bytes 4325376 | tf_op jit(solution)/shard_map/psum | solution.py:100
  9.1 2.1 copy-start.8
  54.0 707.6 %reduce-scatter.3.cloned.1.call-start = ((), (), s32[]{:S(2)}) async-start(), calls=%async_computation.2 | async-start | bytes 270336 | tf_op jit(solution)/shard_map/reduce_scatter | solution.py:120
  54.7 477.5 %copy-start.9 = (f32[64,64]{1,0:T(8,128)}, f32[64,64]{1,0:T(8,128)S(1)}, u32[]{:S(2)}) copy-start(f32[64,64]{1,0:T(8,128)S(1)} %fusion.228) | copy-start | bytes 49156
  210.0 2.8 copy-start.2
  238.1 3.3 copy-start.6
  291.5 12.0 copy-start.7
  303.5 15.2 copy-start.10
  327.4 3.4 copy-start.5
  630.6 642.1 %reduce-scatter.5.cloned.1.call-start = ((), (), s32[]{:S(2)}) async-start(), calls=%async_computation.3 | async-start | bytes 270336 | tf_op jit(solution)/shard_map/reduce_scatter | solution.py:120
  836.1 3.4 copy-start.4
  1347.1 3.4 copy-start.3
  1631.6 5.7 copy-start.1
Sparse Core Ops, SparseCore 0:
  54.2 137.4 all-reduce.11
  630.7 130.9 reduce-scatter.2
  1141.9 130.8 reduce-scatter.4
